TPU v7x, 32 devices: a whole 2x2x4 slice. The times are simulated.
32 devices in a mesh: seabed: 8 (over y, x, core), freq: 4 (over z).
Axes of the slice: x: 2, y: 2, z: 4, core: 2. Of those that a mesh axis runs over, the one named last changes fastest.
Arguments:
- uplift: bfloat16 [128, 32, 40, 128], P('freq', None, 'seabed'), may hold values from -6 to 6
- coefficient: float32 [40, 128], P('seabed'), may hold values from 0.06 to 0.24
- transfer: float32 [4, 2, 600, 5120], P('freq', None, None, 'seabed'), may hold values from -0.0625 to 0.0625
Outputs:
- sensors: float32 [128, 4, 2, 600], P('seabed', 'freq')
All inputs are finite; a program needn't handle non-finite values.
Results may differ from a plain program's by a relative error of at most 0.0003.
Values sent between devices are 32-bit elements; how exact they have to be, the bound alone decides.
No kernel may reach another device: no remote copies, remote signals or barrier semaphores. Data moves between devices by JAX's collectives and lax.ppermute only.
A program may use at most 64 MiB of HBM per device.

v0:
```python
import math
import jax
import jax.numpy as jnp
from jax import lax
from jax.sharding import PartitionSpec as P

FD = 1
PASSES = 3


def with_halo(block, sides, width):
    for axis, dim in sides:
        count = lax.axis_size(axis)
        forward = [(i, i + 1) for i in range(count - 1)]
        backward = [(target, source) for source, target in forward]
        low = lax.ppermute(
            lax.slice_in_dim(block, block.shape[dim] - width, None, axis=dim), axis, forward
        )
        high = lax.ppermute(lax.slice_in_dim(block, 0, width, axis=dim), axis, backward)
        block = jnp.concatenate([low, block, high], axis=dim)
    return block


def dft_table(steps_count, freq_count):
    times = jnp.arange(steps_count, dtype=jnp.int32)
    freqs = jnp.arange(freq_count, dtype=jnp.int32)
    phase = (freqs[:, None] * times[None, :] % steps_count).astype(jnp.float32) * (
        2.0 * math.pi / steps_count
    )
    scale = 1.0 / math.sqrt(steps_count)
    return (
        jnp.stack([jnp.cos(phase), -jnp.sin(phase)], 1).reshape(2 * freq_count, steps_count) * scale
    )


def relax(extended, rows_coefficient):
    centre = extended[:, :, 1:-1]
    padded = jnp.pad(centre, ((0, 0), (0, 0), (0, 0), (1, 1)))
    beside = extended[:, :, 2:] + extended[:, :, :-2] + padded[:, :, :, 2:] + padded[:, :, :, :-2]
    return centre + rows_coefficient * (beside - 4.0 * centre)


def shards(uplift, coefficient, transfer):
    field = uplift.astype(jnp.float32)
    vectors, steps_count, rows, width = field.shape
    extended = with_halo(field, (("seabed", 2),), PASSES)
    coefficient_rim = with_halo(coefficient, (("seabed", 0),), PASSES - 1)
    for step in range(PASSES):
        span = rows + 2 * (PASSES - 1 - step)
        extended = relax(extended, coefficient_rim[step : step + span])
    field = extended
    flat = field.reshape(vectors, steps_count, rows * width)
    freq_count = FD * lax.axis_size("freq")
    table = dft_table(steps_count, freq_count)
    spectrum = jnp.einsum("ft,vtc->fvc", table, flat, precision=lax.Precision.HIGHEST)
    spectrum = spectrum.reshape(freq_count, 2, vectors, rows * width)
    regrouped = lax.all_to_all(spectrum, "freq", split_axis=0, concat_axis=2, tiled=True)
    products = jnp.einsum("kbvc,kasc->vkbas", regrouped, transfer, precision=lax.Precision.HIGHEST)
    real_part = products[:, :, 0, 0] - products[:, :, 1, 1]
    imag_part = products[:, :, 1, 0] + products[:, :, 0, 1]
    return lax.psum_scatter(
        jnp.stack([real_part, imag_part], 2), "seabed", scatter_dimension=0, tiled=True
    )


def solution(mesh):
    placed = (P("freq", None, "seabed", None), P("seabed", None), P("freq", None, None, "seabed"))
    return jax.shard_map(
        shards,
        mesh=mesh,
        in_specs=placed,
        out_specs=P("seabed", "freq", None, None),
        check_vma=False,
    )
```

profile of v0, /device:TPU:0, one launch (start us, length us, event | category | flops | bytes accessed | tf_op | source)
XLA Modules:
  0.0 159.0 jit_solution(17470392824723948402)
XLA Ops:
  6.5 0.0 copy-start
  6.5 0.0 copy-start.2
  6.5 0.0 all-reduce.6.cloned.1.call-start
  6.5 0.0 copy-start.1
  6.5 2.0 %fusion.34 = (f32[32,32,3,128]{3,1,2,0:T(8,128)S(1)}, f32[32,32,3,128]{3,1,2,0:T(8,128)S(1)}) fusion(bf16[32,32,5,128]{3,1,2,0:T(8,128)(2,1)} %param.3), kind=kLoop, calls=%fused_computation.51 | loop fusion | bytes 6291456 | tf_op jit(solution)/shard_map/slice | solution.py:17
  8.5 2.5 %collective-permute-start = (f32[32,32,3,128]{3,1,2,0:T(8,128)S(1)}, f32[32,32,3,128]{3,1,2,0:T(8,128)S(1)}, u32[]{:S(2)}, u32[]{:S(2)}) collective-permute-start(f32[32,32,3,128]{3,1,2,0:T(8,128)S(1)} %get-tuple-element.5), channel_id=1, source_target_pairs={{0,4},{4,8},{8,12},{12,16},{16,20},{20,24},{24,28},{1,5},{5,9},{9,... | collective-permute-start | bytes 4718600 | tf_op jit(solution)/shard_map/ppermute | solution.py:16
  11.0 1.3 collective-permute-start.1
  12.3 0.0 copy-done.2
  12.3 5.0 %collective-permute-start.2 = (f32[2,128]{1,0:T(2,128)S(1)}, f32[2,128]{1,0:T(2,128)S(1)}, u32[]{:S(2)}, u32[]{:S(2)}) collective-permute-start(f32[2,128]{1,0:T(2,128)S(1)} %get-tuple-element.9), channel_id=1, source_target_pairs={{0,4},{4,8},{8,12},{12,16},{16,20},{20,24},{24,28},{1,5},{5,9},{9,... | collective-permute-start | bytes 3080 | tf_op jit(solution)/shard_map/ppermute | solution.py:16
  17.4 1.3 collective-permute-start.3
  18.7 0.1 sine_negate_fusion
  18.7 0.0 copy-done.1
  18.7 0.4 convert_element_type.26
  19.1 0.0 collective-permute-done.2
  19.1 2.6 %collective-permute-done.3 = f32[2,128]{1,0:T(2,128)S(1)} collective-permute-done((f32[2,128]{1,0:T(2,128)S(1)}, f32[2,128]{1,0:T(2,128)S(1)}, u32[]{:S(2)}, u32[]{:S(2)}) %collective-permute-start.3) | collective-permute-done | bytes 1056 | tf_op jit(solution)/shard_map/ppermute | solution.py:19
  21.7 0.0 collective-permute-done
  21.7 0.0 collective-permute-done.1
  21.7 0.7 pad_maximum_fusion
  22.4 0.5 slice.98
  22.9 2.6 %fusion.4 = f32[32,32,9,128]{3,1,2,0:T(8,128)S(1)} fusion(f32[32,32,9,128]{3,1,2,0:T(8,128)S(1)} %slice.98, f32[32,32,11,128]{3,1,2,0:T(8,128)S(1)} %pad_maximum_fusion, f32[9,128]{1,0:T(8,128)S(1)} %pad_maximum_fusion.2), kind=kLoop, calls=%fused_computation.11 | loop fusion | flops 8257536 | bytes 18878976 | tf_op jit(solution)/shard_map/add | solution.py:40
  25.6 0.4 slice.101
  26.0 2.1 %fusion.9 = f32[32,32,7,128]{3,1,2,0:T(8,128)S(1)} fusion(f32[32,32,7,128]{3,1,2,0:T(8,128)S(1)} %slice.101, f32[32,32,9,128]{3,1,2,0:T(8,128)S(1)} %fusion.4, f32[7,128]{1,0:T(8,128)S(1)} %slice.102), kind=kLoop, calls=%fused_computation.17 | loop fusion | flops 6422528 | bytes 14683648 | tf_op jit(solution)/shard_map/add | solution.py:40
  28.0 0.2 slice.105
  28.3 1.4 fusion.16
  29.7 4.2 %copy.8 = f32[32,32,5,128]{3,2,1,0:T(8,128)} copy(f32[32,32,5,128]{3,1,2,0:T(8,128)S(1)} %fusion.16) | data formatting | bytes 5242880 | tf_op jit(solution)/shard_map/add | solution.py:40
  33.9 4.7 %reshape.136 = f32[32,32,640,1]{2,1,0,3:T(8,128)} reshape(f32[32,32,5,128]{3,2,1,0:T(8,128)} %copy.8) | data formatting | bytes 5242880 | tf_op jit(solution)/shard_map/reshape | solution.py:52
  38.6 3.2 %fusion.23 = f32[4,2,32,640]{3,0,2,1:T(4,128)S(1)} fusion(f32[32,32,640,1]{2,1,0,3:T(8,128)} %reshape.136, f32[4,1,32]{2,0,1:T(4,128)S(1)} %get-tuple-element.11, f32[4,1,32]{2,0,1:T(4,128)S(1)} %get-tuple-element.12), kind=kOutput, calls=%fused_computation.36 | convolution fusion | flops 62915072 | bytes 3277824 | tf_op jit(solution)/shard_map/ft,vtc->fvc/dot_general | solution.py:55
  41.9 16.4 %all_to_all.15 = f32[4,2,32,640]{3,2,1,0:T(8,128)S(1)} all-to-all(f32[4,2,32,640]{3,2,1,0:T(8,128)S(1)} %copy.9), channel_id=1, replica_groups=mesh['seabed'=8,'freq'=4] {'freq'}, dimensions={0} | all-to-all | bytes 1310720 | tf_op jit(solution)/shard_map/all_to_all | solution.py:57
  58.3 0.0 copy-done
  58.3 3.1 %fusion.17 = f32[128,1,2,2,600]{0,4,3,2,1:T(8,128)S(1)} fusion(f32[2,128,640,1]{2,1,3,0:T(8,128)S(1)} %bitcast.33, f32[1,2,600,640]{3,2,1,0:T(8,128)S(1)} %copy-done), kind=kOutput, calls=%fused_computation.27 | convolution fusion | flops 2359296000 | bytes 4956160 | tf_op jit(solution)/shard_map/kbvc,kasc->vkbas/dot_general | solution.py:58
  61.5 0.0 copy-start.3
  61.5 0.1 fusion.21
  61.5 0.9 pad_maximum_fusion.1
  62.4 2.1 %copy.11 = f32[128,1,2,600]{3,2,1,0:T(2,128)} copy(f32[128,1,2,600]{0,3,2,1:T(8,128)} %pad_maximum_fusion.1) | data formatting | bytes 1228800 | tf_op jit(solution)/shard_map/stack | solution.py:62
  64.5 0.0 all-reduce.6.cloned.1.call-update
  64.5 0.0 copy-done.3
  64.5 0.6 dynamic-slice
  65.8 84.9 %all-reduce.6.cloned.1.call-done = f32[128,1,2,600]{3,2,1,0:T(2,128)} async-done(((f32[128,1,2,600]{3,2,1,0:T(2,128)}), f32[128,1,2,600]{3,2,1,0:T(2,128)}) %all-reduce.6.cloned.1.call-update) | async-done | bytes 614416
  150.7 1.5 constant_dynamic-slice_fusion
  (5 shorter events, 0.1 us)
Async XLA Ops:
  6.5 51.8 %copy-start = (f32[1,2,600,640]{3,2,1,0:T(8,128)S(1)}, f32[1,2,600,640]{3,2,1,0:T(8,128)}, u32[]{:S(2)}) copy-start(f32[1,2,600,640]{3,2,1,0:T(8,128)} %param.5) | copy-start | bytes 9216004
  6.5 5.8 %copy-start.2 = (f32[5,128]{1,0:T(8,128)S(1)}, f32[5,128]{1,0:T(8,128)}, u32[]{:S(2)}) copy-start(f32[5,128]{1,0:T(8,128)} %param.4) | copy-start | bytes 7684
  6.5 144.1 %all-reduce.6.cloned.1.call-start = ((), (), s32[]{:S(2)}) async-start(), calls=%async_computation.1 | async-start | bytes 1310720
  6.5 12.2 %copy-start.1 = (bf16[32,32,5,128]{3,1,2,0:T(8,128)(2,1)S(1)}, bf16[32,32,5,128]{3,1,2,0:T(8,128)(2,1)}, u32[]{:S(2)}) copy-start(bf16[32,32,5,128]{3,1,2,0:T(8,128)(2,1)} %param.3) | copy-start | bytes 3932164
  8.5 13.2 %collective-permute-start = (f32[32,32,3,128]{3,1,2,0:T(8,128)S(1)}, f32[32,32,3,128]{3,1,2,0:T(8,128)S(1)}, u32[]{:S(2)}, u32[]{:S(2)}) collective-permute-start(f32[32,32,3,128]{3,1,2,0:T(8,128)S(1)} %get-tuple-element.5), channel_id=1, source_target_pairs={{0,4},{4,8},{8,12},{12,16},{16,20},{20,24},{24,28},{1,5},{5,9},{9,... | collective-permute-start | bytes 4718600 | tf_op jit(solution)/shard_map/ppermute | solution.py:16
  11.0 10.7 %collective-permute-start.1 = (f32[32,32,3,128]{3,1,2,0:T(8,128)S(1)}, f32[32,32,3,128]{3,1,2,0:T(8,128)S(1)}, u32[]{:S(2)}, u32[]{:S(2)}) collective-permute-start(f32[32,32,3,128]{3,1,2,0:T(8,128)S(1)} %get-tuple-element.6), channel_id=1, source_target_pairs={{4,0},{8,4},{12,8},{16,12},{20,16},{24,20},{28,24},{5,1},{9,5},{13... | collective-permute-start | bytes 4718600 | tf_op jit(solution)/shard_map/ppermute | solution.py:19
  12.3 6.8 %collective-permute-start.2 = (f32[2,128]{1,0:T(2,128)S(1)}, f32[2,128]{1,0:T(2,128)S(1)}, u32[]{:S(2)}, u32[]{:S(2)}) collective-permute-start(f32[2,128]{1,0:T(2,128)S(1)} %get-tuple-element.9), channel_id=1, source_target_pairs={{0,4},{4,8},{8,12},{12,16},{16,20},{20,24},{24,28},{1,5},{5,9},{9,... | collective-permute-start | bytes 3080 | tf_op jit(solution)/shard_map/ppermute | solution.py:16
  17.4 4.3 %collective-permute-start.3 = (f32[2,128]{1,0:T(2,128)S(1)}, f32[2,128]{1,0:T(2,128)S(1)}, u32[]{:S(2)}, u32[]{:S(2)}) collective-permute-start(f32[2,128]{1,0:T(2,128)S(1)} %get-tuple-element.10), channel_id=1, source_target_pairs={{4,0},{8,4},{12,8},{16,12},{20,16},{24,20},{28,24},{5,1},{9,5},{13... | collective-permute-start | bytes 3080 | tf_op jit(solution)/shard_map/ppermute | solution.py:19
  61.5 3.1 %copy-start.3 = (u32[32]{0:T(128)S(1)}, u32[32]{0:T(128)}, u32[]{:S(2)}) copy-start(u32[32]{0:T(128)} %constant.37) | copy-start | bytes 388
Sparse Core Ops, SparseCore 0:
  64.6 85.9 all-reduce.5
where the time goes:
time: 159 us
  waiting for transfers between devices  87.5 us (55%)
  blocking collectives  16.4 us (10%)
  local copies, waits for them, and re-layouts  16.3 us (10%)
  between operations  14.3 us (9%)
  starting transfers between devices  10.1 us (6%)
  other arithmetic  8.15 us (5%)
  matrix products  6.35 us (4%)
    unnamed x2, waiting for transfers between devices  84.9 us
    all_to_all x1, blocking collectives, shards(): lax.all_to_all(spectrum, 'freq', split_axis=0, concat_axis=2, tiled=True)  16.4 us
    ppermute x2, starting transfers between devices, with_halo(): lax.ppermute(lax.slice_in_dim(block, block.shape[dim] - width, None, axis...  7.52 us
    add x3, other arithmetic, relax(): return centre + rows_coefficient * (beside - 4.0 * centre)  6.11 us
    reshape x1, local copies, waits for them, and re-layouts, shards(): flat = field.reshape(vectors, steps_count, rows * width)  4.7 us
    add x1, local copies, waits for them, and re-layouts, relax(): return centre + rows_coefficient * (beside - 4.0 * centre)  4.19 us
    dot_general x1, matrix products, shards(): jnp.einsum('ft,vtc->fvc', table, flat, precision=lax.Precision.HIGHEST)  3.21 us
  transfers between devices with their start and end apart: 5, of which 2 were waited for; matrix products, arithmetic and copies ran while one was open for 1% of the time, Pallas kernels for 0%

commit v1 on v0

--- a/solution.py
+++ b/solution.py
@@ -54,7 +54,10 @@
     table = dft_table(steps_count, freq_count)
     spectrum = jnp.einsum("ft,vtc->fvc", table, flat, precision=lax.Precision.HIGHEST)
     spectrum = spectrum.reshape(freq_count, 2, vectors, rows * width)
-    regrouped = lax.all_to_all(spectrum, "freq", split_axis=0, concat_axis=2, tiled=True)
+    size = lax.axis_size("freq")
+    blocks = jnp.stack(jnp.split(spectrum, size, axis=0), axis=0)
+    blocks = lax.all_to_all(blocks, "freq", split_axis=0, concat_axis=0)
+    regrouped = jnp.concatenate(blocks, axis=2)
     products = jnp.einsum("kbvc,kasc->vkbas", regrouped, transfer, precision=lax.Precision.HIGHEST)
     real_part = products[:, :, 0, 0] - products[:, :, 1, 1]
     imag_part = products[:, :, 1, 0] + products[:, :, 0, 1]

time: 159 us -> 149 us (0.937)
  local copies, waits for them, and re-layouts: 16.3 us -> 7.54 us
    reshape x1 -> x0, local copies, waits for them, and re-layouts: 4.7 us -> none  [shards(): flat = field.reshape(vectors, steps_count, rows * width)]
    add x1 -> x0, local copies, waits for them, and re-layouts: 4.19 us -> none  [relax(): return centre + rows_coefficient * (beside - 4.0 * centre)]
    add x3 -> x2, other arithmetic: 6.11 us -> 4.71 us  [relax(): return centre + rows_coefficient * (beside - 4.0 * centre)]
where the time goes in v1:
time: 149 us; the launch traced here: 148 us
  waiting for transfers between devices  87.5 us (59%)
  blocking collectives  16.4 us (11%)
  between operations  14.3 us (10%)
  starting transfers between devices  10.1 us (7%)
  local copies, waits for them, and re-layouts  7.54 us (5%)
  other arithmetic  7.01 us (5%)
  matrix products  5.66 us (4%)
    unnamed x2, waiting for transfers between devices  84.9 us
    all_to_all x1, blocking collectives, shards(): blocks = lax.all_to_all(blocks, 'freq', split_axis=0, concat_axis=0)  16.4 us
    ppermute x2, starting transfers between devices, with_halo(): lax.ppermute(lax.slice_in_dim(block, block.shape[dim] - width, None, axis...  7.52 us
    add x2, other arithmetic, relax(): return centre + rows_coefficient * (beside - 4.0 * centre)  4.71 us
    dot_general x1, matrix products, shards(): jnp.einsum('kbvc,kasc->vkbas', regrouped, transfer, precision=lax.Precisi...  3.14 us
  transfers between devices with their start and end apart: 5, of which 2 were waited for; matrix products, arithmetic and copies ran while one was open for 1% of the time, Pallas kernels for 0%

profile of v1, /device:TPU:0, one launch (start us, length us, event | category | flops | bytes accessed | tf_op | source)
XLA Modules:
  0.0 148.4 jit_solution(7739391057713477806)
XLA Ops:
  6.5 0.0 copy-start
  6.5 0.0 copy-start.2
  6.5 0.0 all-reduce.6.cloned.1.call-start
  6.5 0.0 copy-start.1
  6.5 2.0 %fusion.31 = (f32[32,32,3,128]{3,1,2,0:T(8,128)S(1)}, f32[32,32,3,128]{3,1,2,0:T(8,128)S(1)}) fusion(bf16[32,32,5,128]{3,1,2,0:T(8,128)(2,1)} %param.3), kind=kLoop, calls=%fused_computation.54 | loop fusion | bytes 6291456 | tf_op jit(solution)/shard_map/slice | solution.py:17
  8.5 2.5 %collective-permute-start = (f32[32,32,3,128]{3,1,2,0:T(8,128)S(1)}, f32[32,32,3,128]{3,1,2,0:T(8,128)S(1)}, u32[]{:S(2)}, u32[]{:S(2)}) collective-permute-start(f32[32,32,3,128]{3,1,2,0:T(8,128)S(1)} %get-tuple-element.5), channel_id=1, source_target_pairs={{0,4},{4,8},{8,12},{12,16},{16,20},{20,24},{24,28},{1,5},{5,9},{9,... | collective-permute-start | bytes 4718600 | tf_op jit(solution)/shard_map/ppermute | solution.py:16
  11.0 1.3 collective-permute-start.1
  12.3 0.0 copy-done.2
  12.3 5.0 %collective-permute-start.2 = (f32[2,128]{1,0:T(2,128)S(1)}, f32[2,128]{1,0:T(2,128)S(1)}, u32[]{:S(2)}, u32[]{:S(2)}) collective-permute-start(f32[2,128]{1,0:T(2,128)S(1)} %get-tuple-element.13), channel_id=1, source_target_pairs={{0,4},{4,8},{8,12},{12,16},{16,20},{20,24},{24,28},{1,5},{5,9},{9,... | collective-permute-start | bytes 3080 | tf_op jit(solution)/shard_map/ppermute | solution.py:16
  17.4 1.3 collective-permute-start.3
  18.7 0.1 sine_negate_fusion
  18.7 0.0 copy-done.1
  18.7 0.4 convert_element_type.26
  19.1 0.0 collective-permute-done.2
  19.1 2.5 %collective-permute-done.3 = f32[2,128]{1,0:T(2,128)S(1)} collective-permute-done((f32[2,128]{1,0:T(2,128)S(1)}, f32[2,128]{1,0:T(2,128)S(1)}, u32[]{:S(2)}, u32[]{:S(2)}) %collective-permute-start.3) | collective-permute-done | bytes 1056 | tf_op jit(solution)/shard_map/ppermute | solution.py:19
  21.7 0.0 collective-permute-done
  21.7 0.0 collective-permute-done.1
  21.7 0.6 pad_maximum_fusion
  22.4 0.5 slice.102
  22.9 2.6 %fusion.4 = f32[32,32,9,128]{3,1,2,0:T(8,128)S(1)} fusion(f32[32,32,9,128]{3,1,2,0:T(8,128)S(1)} %slice.102, f32[32,32,11,128]{3,1,2,0:T(8,128)S(1)} %pad_maximum_fusion, f32[9,128]{1,0:T(8,128)S(1)} %pad_maximum_fusion.3), kind=kLoop, calls=%fused_computation.11 | loop fusion | flops 8257536 | bytes 18878976 | tf_op jit(solution)/shard_map/add | solution.py:40
  25.5 0.4 slice.105
  25.9 2.1 %fusion.9 = f32[32,32,7,128]{3,1,2,0:T(8,128)S(1)} fusion(f32[32,32,7,128]{3,1,2,0:T(8,128)S(1)} %slice.105, f32[32,32,9,128]{3,1,2,0:T(8,128)S(1)} %fusion.4, f32[7,128]{1,0:T(8,128)S(1)} %slice.106), kind=kLoop, calls=%fused_computation.17 | loop fusion | flops 6422528 | bytes 14683648 | tf_op jit(solution)/shard_map/add | solution.py:40
  28.0 0.2 slice.109
  28.3 2.5 %fusion.18 = f32[8,32,640]{2,0,1:T(8,128)S(1)} fusion(f32[8,32,1]{1,0,2:T(8,128)S(1)} %bitcast.42, f32[32,32,5,128]{3,1,2,0:T(8,128)S(1)} %slice.109, f32[32,32,7,128]{3,1,2,0:T(8,128)S(1)} %fusion.9, f32[5,128]{1,0:T(8,128)S(1)} %copy-done.2), kind=kOutput, calls=%fused_computation.27 | convolution fusion | flops 67502080 | bytes 8527872 | tf_op jit(solution)/shard_map/ft,vtc->fvc/dot_general | solution.py:55
  30.8 0.2 slice_bitcast_fusion.3
  31.0 0.3 pad_maximum_fusion.1
  31.3 16.4 %all_to_all.5 = f32[4,1,2,32,640]{4,2,3,1,0:T(2,128)S(1)} all-to-all(f32[4,1,2,32,640]{4,2,3,1,0:T(2,128)S(1)} %pad_maximum_fusion.1), channel_id=1, replica_groups=mesh['seabed'=8,'freq'=4] {'freq'}, dimensions={0} | all-to-all | bytes 1310720 | tf_op jit(solution)/shard_map/all_to_all | solution.py:59
  47.7 0.0 copy-done
  47.7 3.1 %fusion.21 = f32[128,1,2,2,600]{0,4,3,2,1:T(8,128)S(1)} fusion(f32[1,2,600,640]{3,2,1,0:T(8,128)S(1)} %copy-done, f32[2,128,640,1]{2,0,1,3:T(2,128)S(1)} %bitcast.41), kind=kOutput, calls=%fused_computation.31 | convolution fusion | flops 2359296000 | bytes 4956160 | tf_op jit(solution)/shard_map/kbvc,kasc->vkbas/dot_general | solution.py:61
  50.8 0.0 copy-start.3
  50.9 0.1 fusion.26
  50.9 0.9 pad_maximum_fusion.2
  51.8 2.1 %copy.18 = f32[128,1,2,600]{3,2,1,0:T(2,128)} copy(f32[128,1,2,600]{0,3,2,1:T(8,128)} %pad_maximum_fusion.2) | data formatting | bytes 1228800 | tf_op jit(solution)/shard_map/stack | solution.py:65
  53.9 0.0 all-reduce.6.cloned.1.call-update
  53.9 0.0 copy-done.3
  53.9 0.6 dynamic-slice
  55.1 84.9 %all-reduce.6.cloned.1.call-done = f32[128,1,2,600]{3,2,1,0:T(2,128)} async-done(((f32[128,1,2,600]{3,2,1,0:T(2,128)}), f32[128,1,2,600]{3,2,1,0:T(2,128)}) %all-reduce.6.cloned.1.call-update) | async-done | bytes 614416
  140.0 1.5 %constant_dynamic-slice_fusion = f32[16,1,2,600]{3,2,1,0:T(2,128)} fusion(f32[128,1,2,600]{3,2,1,0:T(2,128)} %all-reduce.6.cloned.1.call-done, u32[]{:T(128)S(6)} %multiply.1), kind=kLoop, calls=%fused_computation.53 | loop fusion | bytes 153604
  (5 shorter events, 0.0 us)
Async XLA Ops:
  6.5 41.2 %copy-start = (f32[1,2,600,640]{3,2,1,0:T(8,128)S(1)}, f32[1,2,600,640]{3,2,1,0:T(8,128)}, u32[]{:S(2)}) copy-start(f32[1,2,600,640]{3,2,1,0:T(8,128)} %param.5) | copy-start | bytes 9216004
  6.5 5.8 %copy-start.2 = (f32[5,128]{1,0:T(8,128)S(1)}, f32[5,128]{1,0:T(8,128)}, u32[]{:S(2)}) copy-start(f32[5,128]{1,0:T(8,128)} %param.4) | copy-start | bytes 7684
  6.5 133.5 %all-reduce.6.cloned.1.call-start = ((), (), s32[]{:S(2)}) async-start(), calls=%async_computation.1 | async-start | bytes 1310720
  6.5 12.2 %copy-start.1 = (bf16[32,32,5,128]{3,1,2,0:T(8,128)(2,1)S(1)}, bf16[32,32,5,128]{3,1,2,0:T(8,128)(2,1)}, u32[]{:S(2)}) copy-start(bf16[32,32,5,128]{3,1,2,0:T(8,128)(2,1)} %param.3) | copy-start | bytes 3932164
  8.5 13.2 %collective-permute-start = (f32[32,32,3,128]{3,1,2,0:T(8,128)S(1)}, f32[32,32,3,128]{3,1,2,0:T(8,128)S(1)}, u32[]{:S(2)}, u32[]{:S(2)}) collective-permute-start(f32[32,32,3,128]{3,1,2,0:T(8,128)S(1)} %get-tuple-element.5), channel_id=1, source_target_pairs={{0,4},{4,8},{8,12},{12,16},{16,20},{20,24},{24,28},{1,5},{5,9},{9,... | collective-permute-start | bytes 4718600 | tf_op jit(solution)/shard_map/ppermute | solution.py:16
  11.0 10.7 %collective-permute-start.1 = (f32[32,32,3,128]{3,1,2,0:T(8,128)S(1)}, f32[32,32,3,128]{3,1,2,0:T(8,128)S(1)}, u32[]{:S(2)}, u32[]{:S(2)}) collective-permute-start(f32[32,32,3,128]{3,1,2,0:T(8,128)S(1)} %get-tuple-element.6), channel_id=1, source_target_pairs={{4,0},{8,4},{12,8},{16,12},{20,16},{24,20},{28,24},{5,1},{9,5},{13... | collective-permute-start | bytes 4718600 | tf_op jit(solution)/shard_map/ppermute | solution.py:19
  12.3 6.8 %collective-permute-start.2 = (f32[2,128]{1,0:T(2,128)S(1)}, f32[2,128]{1,0:T(2,128)S(1)}, u32[]{:S(2)}, u32[]{:S(2)}) collective-permute-start(f32[2,128]{1,0:T(2,128)S(1)} %get-tuple-element.13), channel_id=1, source_target_pairs={{0,4},{4,8},{8,12},{12,16},{16,20},{20,24},{24,28},{1,5},{5,9},{9,... | collective-permute-start | bytes 3080 | tf_op jit(solution)/shard_map/ppermute | solution.py:16
  17.4 4.3 %collective-permute-start.3 = (f32[2,128]{1,0:T(2,128)S(1)}, f32[2,128]{1,0:T(2,128)S(1)}, u32[]{:S(2)}, u32[]{:S(2)}) collective-permute-start(f32[2,128]{1,0:T(2,128)S(1)} %get-tuple-element.14), channel_id=1, source_target_pairs={{4,0},{8,4},{12,8},{16,12},{20,16},{24,20},{28,24},{5,1},{9,5},{13... | collective-permute-start | bytes 3080 | tf_op jit(solution)/shard_map/ppermute | solution.py:19
  50.8 3.1 %copy-start.3 = (u32[32]{0:T(128)S(1)}, u32[32]{0:T(128)}, u32[]{:S(2)}) copy-start(u32[32]{0:T(128)} %constant.37) | copy-start | bytes 388
Sparse Core Ops, SparseCore 0:
  54.0 85.9 all-reduce.5
